TPU v7x, 128 devices: a whole 4x4x4 slice. The times are simulated.
128 devices in a mesh: sess: 32 (over x, z, core), tp: 4 (over y).
Axes of the slice: x: 4, y: 4, z: 4, core: 2. Of those that a mesh axis runs over, the one named last changes fastest.
Arguments:
- hidden: bfloat16 [16384, 8192], P('sess'), may hold values from -6 to 6
- routes: int32 [16384, 1], replicated, may hold values from 0 to 63; in each aligned block of 512 rows (0 to 511, 512 to 1023, ...) at most 16 rows name the same one
- w_qkv: bfloat16 [8192, 4, 1280], P(None, 'tp'), may hold values from -0.0625 to 0.0625
- b_qkv: float32 [4, 1280], P('tp'), may hold values from -8 to 8
- pool: bfloat16 [512, 4, 64, 256], P('sess', 'tp'), may hold values from -8 to 8
- page_lists: int32 [64, 4, 8], replicated, may hold values from 0 to 511, as said below
Outputs:
- attn_out: bfloat16 [64, 512, 4096], P('sess', None, 'tp')
Inputs may be any that keep to these rules, and one draw needn't show every extreme that they name: `routes`: within the rows of one ingest index no session is named by more than 16 rows, a bound that some block reaches. `page_lists`: page p lies on pool index p // 16. For the sessions of one owner (sessions o * 2 to o * 2 + 1) and one 4 head, the 16 listed pages lie on distinct pool indices, exactly 1 on each of them.
All inputs are finite; a program needn't handle non-finite values.
Results may differ from a plain program's by a relative error of at most 0.0065.
Values may be sent and summed in bfloat16 or wider, within the bound.
A program may use at most 192 MiB of HBM per device.

v0:
```python
import math
import jax
import jax.numpy as jnp
from jax import lax
from jax.sharding import PartitionSpec as P

HD = 128
QPK = 8


def place_rows(part_rows, destination, ranking, per_owner, owners, slot_most):
    owner_of = destination // per_owner
    local_of = destination % per_owner
    target = local_of * (owners * slot_most) + owner_of * slot_most + ranking
    buffer = jnp.zeros((per_owner * owners * slot_most, part_rows.shape[1]), part_rows.dtype)
    buffer = buffer.at[target].set(part_rows)
    return buffer.reshape(per_owner, owners * slot_most, part_rows.shape[1])


def on_device(hidden, routes, w_qkv, b_qkv, pool, page_lists):
    owners = lax.axis_size("sess")
    owner_index = lax.axis_index("sess")
    head_index = lax.axis_index("tp")
    rows_here = hidden.shape[0]
    sessions = page_lists.shape[0]
    per_owner = sessions // owners
    slot_most = 2 * rows_here // sessions
    segment = owners * slot_most
    weights = w_qkv[:, 0, :]
    bias = b_qkv[0]
    scale = 1.0 / math.sqrt(HD)
    session_ids = jnp.arange(sessions, dtype=jnp.int32)
    blocks = routes[:, 0].reshape(owners, rows_here)
    destination = lax.dynamic_index_in_dim(blocks, owner_index, 0, keepdims=False)
    onehot = (destination[:, None] == session_ids[None, :]).astype(jnp.int32)
    ranking = jnp.sum(jnp.cumsum(onehot, axis=0) * onehot, axis=1) - 1
    my_sessions = owner_index * per_owner + jnp.arange(per_owner, dtype=jnp.int32)
    counts = jnp.sum((blocks[:, :, None] == my_sessions[None, None, :]).astype(jnp.int32), axis=1)
    starts = jnp.cumsum(counts, axis=0) - counts
    offsets = jnp.arange(slot_most, dtype=jnp.int32)
    live = (offsets[None, None, :] < counts.T[:, :, None]).reshape(per_owner, segment)
    position = (starts.T[:, :, None] + offsets[None, None, :]).reshape(per_owner, segment)
    local_rows = jnp.dot(hidden, weights, preferred_element_type=jnp.float32)
    local_rows = (local_rows + bias).astype(jnp.bfloat16)
    sendable = place_rows(local_rows, destination, ranking, per_owner, owners, slot_most)
    qkv = lax.all_to_all(sendable, "sess", split_axis=1, concat_axis=1, tiled=True)
    pool_dev = pool.shape[0]
    kept = page_lists.shape[2]
    requests = per_owner * kept
    page_cap = max(1, requests // owners)
    lists = lax.dynamic_index_in_dim(page_lists, head_index, 1, keepdims=False).reshape(
        owners, requests
    )
    source_dev = lists // pool_dev
    source_slot = lists % pool_dev
    request_ids = jnp.arange(requests, dtype=jnp.int32)
    before = request_ids[None, :] < request_ids[:, None]
    same_dev = source_dev[:, :, None] == source_dev[:, None, :]
    page_rank = jnp.sum((same_dev & before[None]).astype(jnp.int32), axis=2)
    cap_ids = jnp.arange(page_cap, dtype=jnp.int32)
    matched = (source_dev == owner_index)[:, :, None] & (
        page_rank[:, :, None] == cap_ids[None, None, :]
    )
    slot_pick = jnp.sum(jnp.where(matched, source_slot[:, :, None], 0), axis=1).reshape(
        owners * page_cap
    )
    present = jnp.any(matched, axis=1).reshape(owners * page_cap)
    local_pool = pool[:, 0]
    outgoing = jnp.where(present[:, None, None], local_pool[slot_pick], jnp.zeros((), jnp.bfloat16))
    arrived_pages = lax.all_to_all(outgoing, "sess", split_axis=0, concat_axis=0, tiled=True)
    my_dev = lax.dynamic_index_in_dim(source_dev, owner_index, 0, keepdims=False)
    my_rank = lax.dynamic_index_in_dim(page_rank, owner_index, 0, keepdims=False)
    history = arrived_pages[my_dev * page_cap + my_rank].reshape(
        per_owner, kept * pool.shape[2], pool.shape[3]
    )
    kept_tokens = history.shape[1]
    query_cols = QPK * HD
    query = qkv[:, :, :query_cols].reshape(per_owner, segment, QPK, HD)
    keys = jnp.concatenate([history[:, :, :HD], qkv[:, :, query_cols : query_cols + HD]], axis=1)
    values = jnp.concatenate([history[:, :, HD:], qkv[:, :, query_cols + HD :]], axis=1)
    scores = jnp.einsum("bsgd,bnd->bgsn", query, keys, preferred_element_type=jnp.float32) * scale
    recent = live[:, None, :] & (position[:, None, :] <= position[:, :, None])
    allowed = jnp.concatenate(
        [jnp.ones((per_owner, segment, kept_tokens), jnp.bool_), recent], axis=2
    )[:, None]
    scores = jnp.where(allowed, scores, -1e30)
    top = jnp.max(scores, axis=-1, keepdims=True)
    expo = jnp.where(allowed, jnp.exp(scores - top), 0.0)
    probs = (expo / jnp.sum(expo, axis=-1, keepdims=True)).astype(jnp.bfloat16)
    attended = jnp.einsum("bgsn,bnd->bsgd", probs, values, preferred_element_type=jnp.float32)
    attended = jnp.where(live[:, :, None, None], attended, 0.0)
    return attended.reshape(per_owner, segment, query_cols).astype(jnp.bfloat16)


def solution(mesh):
    in_specs = (
        P("sess", None),
        P(),
        P(None, "tp", None),
        P("tp", None),
        P("sess", "tp", None, None),
        P(),
    )
    out_specs = P("sess", None, "tp")
    return jax.shard_map(
        on_device, mesh=mesh, in_specs=in_specs, out_specs=out_specs, check_vma=False
    )
```

profile of v0, /device:TPU:1, one launch (start us, length us, event | category | flops | bytes accessed | tf_op | source)
XLA Modules:
  0.0 129.8 jit_solution(2608155189427158736)
XLA Ops:
  0.0 0.7 constant_dynamic-slice_fusion.1
  0.8 0.1 copy.88
  0.9 0.1 reshape.358
  0.9 0.1 copy.66
  1.0 0.1 convert_reduce_fusion
  1.2 0.1 copy.70
  1.3 0.1 eq.95
  1.3 0.1 fusion.44
  1.5 0.1 fusion.26
  1.6 0.1 reduce_or.14
  1.7 0.1 reduce_sum.57
  1.8 0.1 reduce_sum.58
  2.0 0.1 reduce_or.18
  2.1 0.6 gather_fusion
  2.7 1.1 broadcast_select_fusion
  3.8 9.5 %all-to-all-start = ((bf16[32,64,256]{2,1,0:T(8,128)(2,1)}), bf16[32,64,256]{2,1,0:T(8,128)(2,1)}, u32[]{:S(2)}, u32[]{:S(2)}) async-start(bf16[32,64,256]{2,1,0:T(8,128)(2,1)} %broadcast_select_fusion), calls=%async_computation | async-start | bytes 2097152 | tf_op jit(solution)/shard_map/all_to_all | solution.py:70
  13.3 0.5 broadcast.377
  13.8 0.8 reduce.14
  14.7 17.6 %fusion.13 = bf16[512,1280]{1,0:T(8,128)(2,1)} fusion(bf16[512,8192]{1,0:T(8,128)(2,1)} %param.6, bf16[8192,1,1280]{2,0,1:T(8,128)(2,1)} %param.8, f32[1280]{0:T(1024)S(1)} %reduce.9), kind=kOutput, calls=%fused_computation.17 | convolution fusion | flops 10738728960 | bytes 30675968 | tf_op jit(solution)/shard_map/dot_general | solution.py:43
  32.3 1.2 reduce-window.6
  33.5 0.2 slice_reduce_fusion
  33.8 0.1 fusion.22
  34.0 4.6 %scatter_custom_fusion = bf16[1024,1280]{1,0:T(8,128)(2,1)S(1)} fusion(s32[512]{0:T(512)S(1)} %bitcast.106, bf16[512,1280]{1,0:T(8,128)(2,1)} %fusion.13, bf16[]{:T(256)} %constant.102.clone.1), kind=kCustom, calls=%fused_computation.19 | custom fusion | bytes 2621952 | tf_op jit(solution)/shard_map/scatter | solution.py:16
  38.6 4.2 %copy.72 = bf16[2,512,1280]{2,0,1:T(2,128)(2,1)} copy(bf16[2,512,1280]{2,1,0:T(8,128)(2,1)S(1)} %bitcast.98) | data formatting | bytes 5242880 | tf_op jit(solution)/shard_map/reshape | solution.py:17
  42.8 0.0 all-to-all-done
  42.8 7.4 %all-to-all-start.1 = ((bf16[2,512,1280]{2,0,1:T(2,128)(2,1)}), bf16[2,512,1280]{2,0,1:T(2,128)(2,1)S(1)}, u32[]{:S(2)}, u32[]{:S(2)}) async-start(bf16[2,512,1280]{2,0,1:T(2,128)(2,1)} %copy.72), calls=%async_computation.1 | async-start | bytes 5242880 | tf_op jit(solution)/shard_map/all_to_all | solution.py:46
  50.2 0.1 lt.108
  50.3 0.2 convert_reduce_fusion.1
  50.5 0.1 copy.63
  50.6 0.1 reduce_window_sum.30
  50.6 0.1 copy.64
  50.7 0.1 copy.75
  50.8 0.1 add.190
  50.9 0.1 add.191
  51.0 0.1 lt.110
  51.0 0.1 lt.111
  51.2 0.5 compare_and_fusion
  51.7 1.3 concatenate.10
  53.0 0.2 add_reduce_fusion
  53.2 1.8 %gather_fusion.1 = bf16[16,64,256]{2,1,0:T(8,128)(2,1)S(1)} fusion(bf16[32,64,256]{2,1,0:T(8,128)(2,1)} %all-to-all-done, s32[1024]{0:T(1024)S(1)} %pad_clamp_fusion), kind=kCustom, calls=%fused_computation.1 | custom fusion | bytes 1048640 | tf_op jit(solution)/shard_map/gather | solution.py:73
  55.0 0.8 fusion.47
  55.8 28.3 %all-to-all-done.1 = bf16[2,512,1280]{2,0,1:T(2,128)(2,1)S(1)} async-done(((bf16[2,512,1280]{2,0,1:T(2,128)(2,1)}), bf16[2,512,1280]{2,0,1:T(2,128)(2,1)S(1)}, u32[]{:S(2)}, u32[]{:S(2)}) %all-to-all-start.1) | async-done | bytes 2621472 | tf_op jit(solution)/shard_map/all_to_all | solution.py:46
  84.1 2.8 %slice.37 = bf16[2,512,1024]{2,0,1:T(2,128)(2,1)} slice(bf16[2,512,1280]{2,0,1:T(2,128)(2,1)S(1)} %all-to-all-done.1), slice={[0:2], [0:512], [0:1024]} | slice | bytes 4194304 | tf_op jit(solution)/shard_map/slice | solution.py:78
  86.8 6.1 %copy.91 = bf16[2,512,1024]{1,2,0:T(8,128)(2,1)} copy(bf16[2,512,1024]{2,0,1:T(2,128)(2,1)} %slice.37) | data formatting | bytes 4194304
  93.0 0.4 fusion.46
  93.4 21.9 %fusion.48 = (f32[2,8,512]{2,1,0:T(8,128)S(1)}, f32[2,8,512,1024]{2,3,1,0:T(8,128)}) fusion(bf16[2,512,8,128]{1,3,2,0:T(8,128)(2,1)} %bitcast.99, pred[2,512,1024]{1,2,0:T(8,128)(4,1)} %concatenate.10, bf16[2,512,128]{2,1,0:T(8,128)(2,1)S(1)} %copy.90, bf16[2,512,128]{2,1,0:T(8,128)(2,1)} %get-tuple-element.10), kind=kOutput, calls=%fused_computation.90 | convolution fusion | flops 2190476288 | bytes 37257216 | tf_op jit(solution)/shard_map/sub | solution.py:88
  115.3 12.1 %select_convert_fusion = bf16[2,128,8,512]{3,1,2,0:T(8,128)(2,1)S(1)} fusion(pred[2,512]{1,0:T(4,128)(4,1)S(1)} %broadcast_compare_fusion.1, f32[2,8,512,1024]{2,3,1,0:T(8,128)} %get-tuple-element.12, f32[2,8,512]{2,1,0:T(8,128)S(1)} %get-tuple-element.11, bf16[2,512,128]{2,1,0:T(8,128)(2,1)S(1)} %copy.89, bf16[2,512,128]{2,1,0:T(8,128)(2,1)S(1)} %get-tuple-element.9), kind=kOutput, calls=%fused_computation.15 | convolution fusion | flops 2167406592 | bytes 36209664 | tf_op jit(solution)/shard_map/bgsn,bnd->bsgd/dot_general | solution.py:90
  127.4 2.4 %copy.81 = bf16[2,512,1024]{2,1,0:T(8,128)(2,1)} copy(bf16[2,512,1024]{1,2,0:T(8,128)(2,1)S(1)} %bitcast.100) | data formatting | bytes 4194304 | tf_op jit(solution)/shard_map/convert_element_type | solution.py:92
  (30 shorter events, 0.3 us)
Async XLA Ops:
  0.0 2.1 %copy-start = (bf16[16,1,64,256]{3,2,1,0:T(8,128)(2,1)S(1)}, bf16[16,1,64,256]{3,2,1,0:T(8,128)(2,1)}, u32[]{:S(2)}) copy-start(bf16[16,1,64,256]{3,2,1,0:T(8,128)(2,1)} %param.10) | copy-start | bytes 1572868
  0.0 13.8 %copy-start.2 = (s32[16384,1]{0,1:T(1,128)S(1)}, s32[16384,1]{0,1:T(1,128)}, u32[]{:S(2)}) copy-start(s32[16384,1]{0,1:T(1,128)} %param.7) | copy-start | bytes 196612
  0.0 14.6 %copy-start.3 = (f32[1,1280]{1,0:T(1,128)S(1)}, f32[1,1280]{1,0:T(1,128)}, u32[]{:S(2)}) copy-start(f32[1,1280]{1,0:T(1,128)} %param.9) | copy-start | bytes 15364
  3.8 39.0 %all-to-all-start = ((bf16[32,64,256]{2,1,0:T(8,128)(2,1)}), bf16[32,64,256]{2,1,0:T(8,128)(2,1)}, u32[]{:S(2)}, u32[]{:S(2)}) async-start(bf16[32,64,256]{2,1,0:T(8,128)(2,1)} %broadcast_select_fusion), calls=%async_computation | async-start | bytes 2097152 | tf_op jit(solution)/shard_map/all_to_all | solution.py:70
  42.8 41.3 %all-to-all-start.1 = ((bf16[2,512,1280]{2,0,1:T(2,128)(2,1)}), bf16[2,512,1280]{2,0,1:T(2,128)(2,1)S(1)}, u32[]{:S(2)}, u32[]{:S(2)}) async-start(bf16[2,512,1280]{2,0,1:T(2,128)(2,1)} %copy.72), calls=%async_computation.1 | async-start | bytes 5242880 | tf_op jit(solution)/shard_map/all_to_all | solution.py:46
  115.3 14.5 %copy-start.1 = (bf16[16,1,64,256]{3,2,1,0:T(8,128)(2,1)S(1)}, bf16[16,1,64,256]{3,2,1,0:T(8,128)(2,1)}, u32[]{:S(2)}) copy-start(bf16[16,1,64,256]{3,2,1,0:T(8,128)(2,1)} %param.10) | copy-start | bytes 1572868
where the time goes:
time: 130 us
  matrix products  51.6 us (40%)
  waiting for transfers between devices  28.3 us (22%)
  local copies, waits for them, and re-layouts  27.8 us (21%)
  starting transfers between devices  16.9 us (13%)
  other arithmetic  4.97 us (4%)
    all_to_all x1, waiting for transfers between devices, on_device(): lax.all_to_all(sendable, 'sess', split_axis=1, concat_axis=1, tiled=True)  28.3 us
    sub x1, matrix products, on_device(): expo = jnp.where(allowed, jnp.exp(scores - top), 0.0)  21.9 us
    dot_general x1, matrix products, on_device(): local_rows = jnp.dot(hidden, weights, preferred_element_type=jnp.float32)  17.6 us
    dot_general x1, matrix products, on_device(): jnp.einsum('bgsn,bnd->bsgd', probs, values, preferred_element_type=jnp.fl...  12.1 us
    all_to_all x1, starting transfers between devices, on_device(): lax.all_to_all(outgoing, 'sess', split_axis=0, concat_axis=0, tiled=True)  9.49 us
    all_to_all x1, starting transfers between devices, on_device(): lax.all_to_all(sendable, 'sess', split_axis=1, concat_axis=1, tiled=True)  7.39 us
    unnamed x13, local copies, waits for them, and re-layouts  6.82 us
    scatter x1, local copies, waits for them, and re-layouts, place_rows(): buffer = buffer.at[target].set(part_rows)  4.61 us
  transfers between devices with their start and end apart: 2, of which 1 were waited for; matrix products, arithmetic and copies ran while one was open for 27% of the time, Pallas kernels for 0%

commit v1 on v0

--- a/solution.py
+++ b/solution.py
@@ -43,7 +43,10 @@
     local_rows = jnp.dot(hidden, weights, preferred_element_type=jnp.float32)
     local_rows = (local_rows + bias).astype(jnp.bfloat16)
     sendable = place_rows(local_rows, destination, ranking, per_owner, owners, slot_most)
-    qkv = lax.all_to_all(sendable, "sess", split_axis=1, concat_axis=1, tiled=True)
+    qkv = jnp.concatenate(
+        lax.all_to_all(jnp.stack(jnp.split(sendable, lax.axis_size("sess"), axis=1)), "sess", 0, 0),
+        axis=1,
+    )
     pool_dev = pool.shape[0]
     kept = page_lists.shape[2]
     requests = per_owner * kept

time: 130 us -> 141 us (1.085)
  local copies, waits for them, and re-layouts: 27.8 us -> 37.5 us
    unnamed x13 -> x43, local copies, waits for them, and re-layouts: 6.82 us -> 20.3 us
    reshape x1, local copies, waits for them, and re-layouts: 4.2 us -> 0.17 us  [on_device(): jnp.concatenate(lax.all_to_all(jnp.stack(jnp.split(sendable, lax.axis_siz...]
  transfers between devices with their start and end apart: 2 -> 2, of which waited for: 1 -> 1; matrix products, arithmetic and copies ran while one was open for 27% -> 36% of each run, Pallas kernels for 0% -> 0%
where the time goes in v1:
time: 141 us; the launch traced here: 140 us
  matrix products  51.6 us (37%)
  local copies, waits for them, and re-layouts  37.5 us (27%)
  waiting for transfers between devices  29.1 us (21%)
  starting transfers between devices  16.9 us (12%)
  other arithmetic  4.97 us (4%)
    all_to_all x1, waiting for transfers between devices, on_device(): lax.all_to_all(jnp.stack(jnp.split(sendable, lax.axis_size('sess'), axis=...  29.1 us
    sub x1, matrix products, on_device(): expo = jnp.where(allowed, jnp.exp(scores - top), 0.0)  21.8 us
    unnamed x43, local copies, waits for them, and re-layouts  20.3 us
    dot_general x1, matrix products, on_device(): local_rows = jnp.dot(hidden, weights, preferred_element_type=jnp.float32)  17.6 us
    dot_general x1, matrix products, on_device(): jnp.einsum('bgsn,bnd->bsgd', probs, values, preferred_element_type=jnp.fl...  12.2 us
    all_to_all x1, starting transfers between devices, on_device(): lax.all_to_all(outgoing, 'sess', split_axis=0, concat_axis=0, tiled=True)  9.48 us
    all_to_all x1, starting transfers between devices, on_device(): lax.all_to_all(jnp.stack(jnp.split(sendable, lax.axis_size('sess'), axis=...  7.39 us
    scatter x1, local copies, waits for them, and re-layouts, place_rows(): buffer = buffer.at[target].set(part_rows)  4.43 us
  transfers between devices with their start and end apart: 2, of which 1 were waited for; matrix products, arithmetic and copies ran while one was open for 36% of the time, Pallas kernels for 0%

profile of v1, /device:TPU:1, one launch (start us, length us, event | category | flops | bytes accessed | tf_op | source)
XLA Modules:
  0.0 140.2 jit_solution(6621447532259360711)
XLA Ops:
  0.0 0.7 constant_dynamic-slice_fusion.1
  2.7 1.1 broadcast_select_fusion
  3.8 9.5 %all-to-all-start = ((bf16[32,64,256]{2,1,0:T(8,128)(2,1)}), bf16[32,64,256]{2,1,0:T(8,128)(2,1)}, u32[]{:S(2)}, u32[]{:S(2)}) async-start(bf16[32,64,256]{2,1,0:T(8,128)(2,1)} %broadcast_select_fusion), calls=%async_computation | async-start | bytes 2097152 | tf_op jit(solution)/shard_map/all_to_all | solution.py:73
  13.8 0.8 reduce.14
  14.7 1.2 reduce-window.6
  16.4 17.6 %fusion.13 = bf16[512,1280]{1,0:T(8,128)(2,1)} fusion(bf16[512,8192]{1,0:T(8,128)(2,1)} %param.6, bf16[8192,1,1280]{2,0,1:T(8,128)(2,1)} %param.8, f32[1280]{0:T(1024)S(1)} %reduce.9), kind=kOutput, calls=%fused_computation.17 | convolution fusion | flops 10738728960 | bytes 30675968 | tf_op jit(solution)/shard_map/dot_general | solution.py:43
  34.0 4.4 %scatter_custom_fusion = bf16[1024,1280]{1,0:T(8,128)(2,1)S(1)} fusion(s32[512]{0:T(512)S(1)} %bitcast.270, bf16[512,1280]{1,0:T(8,128)(2,1)} %fusion.13, bf16[]{:T(256)} %constant.102.clone.1), kind=kCustom, calls=%fused_computation.19 | custom fusion | bytes 2621952 | tf_op jit(solution)/shard_map/scatter | solution.py:16
  38.4 0.6 fusion.55
  39.1 0.6 fusion.54
  39.7 0.6 fusion.53
  40.3 0.6 fusion.52
  40.9 0.6 fusion.51
  41.6 0.6 fusion.50
  42.2 0.6 fusion.49
  42.8 0.6 fusion.48
  43.5 0.6 fusion.47
  44.1 0.6 fusion.46
  44.7 0.6 fusion.45
  45.4 0.6 fusion.44
  46.0 0.6 fusion.43
  46.6 0.6 fusion.42
  47.3 0.6 fusion.41
  47.9 0.6 fusion.40
  48.5 0.6 fusion.39
  49.2 0.6 fusion.38
  49.8 0.6 fusion.37
  50.5 0.6 fusion.36
  51.1 0.6 fusion.35
  51.7 0.6 fusion.34
  52.4 0.6 fusion.33
  53.0 0.6 fusion.32
  53.6 0.6 fusion.31
  54.3 0.6 fusion.30
  54.9 0.6 fusion.29
  55.5 0.6 fusion.28
  56.2 0.6 fusion.27
  56.8 0.6 fusion.26
  57.4 0.6 fusion.25
  58.1 0.6 fusion.24
  58.7 7.4 %all-to-all-start.1 = ((bf16[32,2,16,1280]{3,2,1,0:T(8,128)(2,1)}), bf16[32,2,16,1280]{3,2,1,0:T(8,128)(2,1)S(1)}, u32[]{:S(2)}, u32[]{:S(2)}) async-start(bf16[32,2,16,1280]{3,2,1,0:T(8,128)(2,1)} %fusion.24), calls=%async_computation.1 | async-start | bytes 5242880 | tf_op jit(solution)/shard_map/all_to_all | solution.py:47
  67.6 1.3 concatenate.10
  69.1 1.8 %gather_fusion.1 = bf16[16,64,256]{2,1,0:T(8,128)(2,1)S(1)} fusion(bf16[32,64,256]{2,1,0:T(8,128)(2,1)} %all-to-all-done, s32[1024]{0:T(1024)S(1)} %pad_clamp_fusion), kind=kCustom, calls=%fused_computation.1 | custom fusion | bytes 1048640 | tf_op jit(solution)/shard_map/gather | solution.py:76
  70.9 29.1 %all-to-all-done.1 = bf16[32,2,16,1280]{3,2,1,0:T(8,128)(2,1)S(1)} async-done(((bf16[32,2,16,1280]{3,2,1,0:T(8,128)(2,1)}), bf16[32,2,16,1280]{3,2,1,0:T(8,128)(2,1)S(1)}, u32[]{:S(2)}, u32[]{:S(2)}) %all-to-all-start.1) | async-done | bytes 2621472 | tf_op jit(solution)/shard_map/all_to_all | solution.py:47
  100.5 0.9 fusion.78
  101.3 2.5 %copy.122 = bf16[2,512,1024]{1,2,0:T(8,128)(2,1)} copy(bf16[2,512,1024]{2,1,0:T(8,128)(2,1)S(1)} %slice.37) | data formatting | bytes 4194304 | tf_op jit(solution)/shard_map/slice | solution.py:81
  103.9 21.8 %fusion.80 = (f32[2,8,512]{2,1,0:T(8,128)S(1)}, f32[2,8,512,1024]{2,3,1,0:T(8,128)}) fusion(bf16[2,512,8,128]{1,3,2,0:T(8,128)(2,1)} %bitcast.263, pred[2,512,1024]{1,2,0:T(8,128)(4,1)} %concatenate.10, bf16[2,512,128]{2,1,0:T(8,128)(2,1)S(1)} %get-tuple-element.8, bf16[2,512,128]{2,1,0:T(8,128)(2,1)S(1)} %copy-done.2), kind=kOutput, calls=%fused_computation.154 | convolution fusion | flops 2190476288 | bytes 37257216 | tf_op jit(solution)/shard_map/sub | solution.py:91
  125.7 12.2 %select_convert_fusion = bf16[2,128,8,512]{3,1,2,0:T(8,128)(2,1)S(1)} fusion(pred[2,512]{1,0:T(4,128)(4,1)S(1)} %broadcast_compare_fusion.1, f32[2,8,512,1024]{2,3,1,0:T(8,128)} %get-tuple-element.12, f32[2,8,512]{2,1,0:T(8,128)S(1)} %get-tuple-element.11, bf16[2,512,128]{2,1,0:T(8,128)(2,1)S(1)} %get-tuple-element.7, ...), kind=kOutput, calls=%fused_computation.15 | convolution fusion | flops 2167406592 | bytes 36209664 | tf_op jit(solution)/shard_map/bgsn,bnd->bsgd/dot_general | solution.py:93
  137.9 2.4 %copy.126 = bf16[2,512,1024]{2,1,0:T(8,128)(2,1)} copy(bf16[2,512,1024]{1,2,0:T(8,128)(2,1)S(1)} %bitcast.264) | data formatting | bytes 4194304 | tf_op jit(solution)/shard_map/convert_element_type | solution.py:95
  (61 shorter events, 5.0 us)
Async XLA Ops:
  0.0 2.1 %copy-start = (bf16[16,1,64,256]{3,2,1,0:T(8,128)(2,1)S(1)}, bf16[16,1,64,256]{3,2,1,0:T(8,128)(2,1)}, u32[]{:S(2)}) copy-start(bf16[16,1,64,256]{3,2,1,0:T(8,128)(2,1)} %param.10) | copy-start | bytes 1572868
  2.7 11.1 %copy-start.3 = (s32[16384,1]{0,1:T(1,128)S(1)}, s32[16384,1]{0,1:T(1,128)}, u32[]{:S(2)}) copy-start(s32[16384,1]{0,1:T(1,128)} %param.7) | copy-start | bytes 196612
  2.7 13.7 %copy-start.4 = (f32[1,1280]{1,0:T(1,128)S(1)}, f32[1,1280]{1,0:T(1,128)}, u32[]{:S(2)}) copy-start(f32[1,1280]{1,0:T(1,128)} %param.9) | copy-start | bytes 15364
  3.8 54.9 %all-to-all-start = ((bf16[32,64,256]{2,1,0:T(8,128)(2,1)}), bf16[32,64,256]{2,1,0:T(8,128)(2,1)}, u32[]{:S(2)}, u32[]{:S(2)}) async-start(bf16[32,64,256]{2,1,0:T(8,128)(2,1)} %broadcast_select_fusion), calls=%async_computation | async-start | bytes 2097152 | tf_op jit(solution)/shard_map/all_to_all | solution.py:73
  58.7 41.3 %all-to-all-start.1 = ((bf16[32,2,16,1280]{3,2,1,0:T(8,128)(2,1)}), bf16[32,2,16,1280]{3,2,1,0:T(8,128)(2,1)S(1)}, u32[]{:S(2)}, u32[]{:S(2)}) async-start(bf16[32,2,16,1280]{3,2,1,0:T(8,128)(2,1)} %fusion.24), calls=%async_computation.1 | async-start | bytes 5242880 | tf_op jit(solution)/shard_map/all_to_all | solution.py:47
  101.3 2.5 %copy-start.2 = (bf16[2,512,128]{2,1,0:T(8,128)(2,1)S(1)}, bf16[2,512,128]{2,1,0:T(8,128)(2,1)}, u32[]{:S(2)}) copy-start(bf16[2,512,128]{2,1,0:T(8,128)(2,1)} %get-tuple-element.13) | copy-start | bytes 786436
  125.7 14.6 %copy-start.1 = (bf16[16,1,64,256]{3,2,1,0:T(8,128)(2,1)S(1)}, bf16[16,1,64,256]{3,2,1,0:T(8,128)(2,1)}, u32[]{:S(2)}) copy-start(bf16[16,1,64,256]{3,2,1,0:T(8,128)(2,1)} %param.10) | copy-start | bytes 1572868
